TPU v7x, 32 devices: a whole 2x2x4 slice. The times are simulated.
32 devices in a mesh: had: 4 (over z), blk: 8 (over y, x, core).
Axes of the slice: x: 2, y: 2, z: 4, core: 2. Of those that a mesh axis runs over, the one named last changes fastest.
Arguments:
- panel: bfloat16 [65536, 512], P(('had', 'blk')), may hold values from -100 to 100
- signs: int32 [65536], P(('had', 'blk')), may hold values from 0 to 1
- sample_rows: int32 [8, 2048], P('blk'), may hold values from 0 to 8191
Outputs:
- q_panel: bfloat16 [65536, 512], P(('had', 'blk'))
- r_sketch: float32 [512, 512], replicated
- r_gram: float32 [512, 512], replicated
All inputs are finite; a program needn't handle non-finite values.
Results may differ from a plain program's by a relative error of at most 0.0075.
The roundings to bfloat16 on the way count: a program that leaves them out, or rounds other values in their place, can miss the bound.
Values sent between devices are 32-bit elements; how exact they have to be, the bound alone decides.
A program may use at most 448 MiB of HBM per device.

v0:
```python
import math

import jax
import jax.numpy as jnp
from jax import lax
from jax.sharding import PartitionSpec as P

LH = 32


def bit_parity(value):
    counted = jnp.zeros_like(value)
    for shift_count in range(16):
        counted = counted + jnp.bitwise_and(jnp.right_shift(value, shift_count), 1)
    return counted % 2


def hadamard(order):
    first = lax.broadcasted_iota(jnp.int32, (order, order), 0)
    second = lax.broadcasted_iota(jnp.int32, (order, order), 1)
    parity = bit_parity(jnp.bitwise_and(first, second))
    return (1 - 2 * parity).astype(jnp.float32)


def upper_factor(matrix):
    return jnp.linalg.cholesky(matrix).T


def lower_inverse(lower):
    order = lower.shape[0]
    inverse = (1.0 / jnp.diagonal(lower)).reshape(order, 1, 1)
    width = 1
    while width < order:
        count = order // (2 * width)
        tiles = lower.reshape(count, 2 * width, count, 2 * width)
        diag_tiles = jnp.moveaxis(jnp.diagonal(tiles, axis1=0, axis2=2), -1, 0)
        corner = diag_tiles[:, width:, :width]
        first_inv = inverse[0::2]
        second_inv = inverse[1::2]
        partial_value = jnp.einsum(
            "ajk,akl->ajl", corner, first_inv, precision=lax.Precision.HIGHEST
        )
        lower_left = -jnp.einsum(
            "aij,ajl->ail", second_inv, partial_value, precision=lax.Precision.HIGHEST
        )
        zero_tile = jnp.zeros_like(corner)
        top_half = jnp.concatenate([first_inv, zero_tile], axis=2)
        bottom_half = jnp.concatenate([lower_left, second_inv], axis=2)
        inverse = jnp.concatenate([top_half, bottom_half], axis=1)
        width = width * 2
    return inverse[0]


def inverse_upper(factor):
    return lower_inverse(factor.T).T


def on_device(panel, signs, sample_rows):
    n_had = lax.axis_size("had")
    n_blk = lax.axis_size("blk")
    my_group = lax.axis_index("had")
    rows_dev, columns = panel.shape
    sketch_count = sample_rows.shape[1]
    groups = rows_dev // LH
    flipped = jnp.where(signs[:, None] == 1, -panel, panel)
    inner = hadamard(LH).astype(jnp.bfloat16)
    mixed = jnp.einsum(
        "ml,glk->gmk",
        inner,
        flipped.reshape(groups, LH, columns),
        preferred_element_type=jnp.float32,
    )
    mixed = mixed.reshape(rows_dev, columns)
    picks = sample_rows[0]
    owners = picks // rows_dev
    offsets = picks % rows_dev
    factor = 1.0 / math.sqrt(n_had * LH * sketch_count * n_blk)
    parity = bit_parity(jnp.bitwise_and(owners, my_group))
    weights = (1 - 2 * parity).astype(jnp.float32) * factor
    partial_sketch = jnp.take(mixed, offsets, axis=0) * weights[:, None]
    sketch = lax.psum(partial_sketch, ("had", "blk"))
    sketch_gram = jnp.dot(
        sketch.T, sketch, precision=lax.Precision.HIGHEST, preferred_element_type=jnp.float32
    )
    r_sketch = upper_factor(sketch_gram)
    sketch_inverse = inverse_upper(r_sketch).astype(jnp.bfloat16)
    whitened = jnp.dot(panel, sketch_inverse, preferred_element_type=jnp.float32).astype(
        jnp.bfloat16
    )
    partial_gram = jnp.einsum("rk,rj->kj", whitened, whitened, preferred_element_type=jnp.float32)
    summed = lax.psum(partial_gram, ("had", "blk"))
    gram_matrix = summed / (rows_dev * n_had * n_blk)
    r_gram = upper_factor(gram_matrix)
    gram_inverse = inverse_upper(r_gram).astype(jnp.bfloat16)
    q_panel = jnp.dot(whitened, gram_inverse, preferred_element_type=jnp.float32).astype(
        jnp.bfloat16
    )
    return (q_panel, r_sketch, r_gram)


def solution(mesh):
    placed = (P(("had", "blk"), None), P(("had", "blk")), P("blk", None))
    return jax.shard_map(
        on_device,
        mesh=mesh,
        in_specs=placed,
        out_specs=(P(("had", "blk"), None), P(), P()),
        check_vma=False,
    )
```

profile of v0, /device:TPU:0, one launch (start us, length us, event | category | flops | bytes accessed | tf_op | source)
XLA Modules:
  0.0 1226.9 jit_solution(7551053319992622696)
XLA Ops:
  12.5 11.7 gather_fusion
  28.4 145.2 %all-reduce.22.cloned.1.call-done = f32[2048,512]{1,0:T(8,128)} async-done(((f32[2048,512]{1,0:T(8,128)}), f32[2048,512]{1,0:T(8,128)}) %all-reduce.22.cloned.1.call-update) | async-done | bytes 4194320 | tf_op jit(solution)/shard_map/psum | solution.py:81
  185.7 11.7 cholesky.286
  209.9 11.7 cholesky.305
  233.4 11.7 cholesky.326
  256.4 11.7 cholesky.343
  278.0 68.4 %reshape.325 = f32[256,2,256,2]{3,2,1,0:T(8,128)} reshape(f32[512,512]{1,0:T(8,128)S(1)} %select_select_fusion.1) | data formatting | bytes 2097152 | tf_op jit(solution)/shard_map/reshape | solution.py:35
  346.4 35.9 %reshape.326 = f32[128,4,128,4]{3,2,1,0:T(8,128)} reshape(f32[512,512]{1,0:T(8,128)S(1)} %select_select_fusion.1) | data formatting | bytes 2097152 | tf_op jit(solution)/shard_map/reshape | solution.py:35
  382.3 11.0 reshape.327
  406.7 107.3 %copy.213 = f32[256,2,256,2]{3,1,2,0:T(2,128)} copy(f32[256,2,256,2]{3,2,1,0:T(8,128)} %reshape.325) | data formatting | bytes 2097152 | tf_op jit(solution)/shard_map/reshape | solution.py:35
  517.3 38.0 %copy.215 = f32[128,4,128,4]{3,1,2,0:T(4,128)} copy(f32[128,4,128,4]{3,2,1,0:T(8,128)} %reshape.326) | data formatting | bytes 2097152 | tf_op jit(solution)/shard_map/reshape | solution.py:35
  559.5 20.5 %copy.217 = f32[64,8,64,8]{3,1,2,0:T(8,128)} copy(f32[64,8,64,8]{3,2,1,0:T(8,128)} %reshape.327) | data formatting | bytes 2097152 | tf_op jit(solution)/shard_map/reshape | solution.py:35
  587.8 14.2 %copy.219 = f32[32,16,32,16]{3,1,2,0:T(8,128)} copy(f32[32,16,32,16]{3,2,1,0:T(8,128)} %reshape.328) | data formatting | bytes 2097152 | tf_op jit(solution)/shard_map/reshape | solution.py:35
  637.0 128.6 %all-reduce.24.cloned.1.call-done = f32[512,512]{0,1:T(8,128)} async-done(((f32[512,512]{0,1:T(8,128)}), f32[512,512]{0,1:T(8,128)}) %all-reduce.24.cloned.1.call-update) | async-done | bytes 1048592 | tf_op jit(solution)/shard_map/psum | solution.py:91
  767.7 11.7 cholesky.358
  790.2 11.7 cholesky.377
  812.5 11.7 cholesky.398
  835.1 11.7 cholesky.415
  857.2 68.4 %reshape.336 = f32[256,2,256,2]{3,2,1,0:T(8,128)} reshape(f32[512,512]{1,0:T(8,128)S(1)} %select_select_fusion) | data formatting | bytes 2097152 | tf_op jit(solution)/shard_map/reshape | solution.py:35
  925.6 35.9 %reshape.337 = f32[128,4,128,4]{3,2,1,0:T(8,128)} reshape(f32[512,512]{1,0:T(8,128)S(1)} %select_select_fusion) | data formatting | bytes 2097152 | tf_op jit(solution)/shard_map/reshape | solution.py:35
  986.3 107.3 %copy.212 = f32[256,2,256,2]{3,1,2,0:T(2,128)} copy(f32[256,2,256,2]{3,2,1,0:T(8,128)} %reshape.336) | data formatting | bytes 2097152 | tf_op jit(solution)/shard_map/reshape | solution.py:35
  1096.9 37.8 %copy.214 = f32[128,4,128,4]{3,1,2,0:T(4,128)} copy(f32[128,4,128,4]{3,2,1,0:T(8,128)} %reshape.337) | data formatting | bytes 2097152 | tf_op jit(solution)/shard_map/reshape | solution.py:35
  1138.9 20.3 %copy.216 = f32[64,8,64,8]{3,1,2,0:T(8,128)} copy(f32[64,8,64,8]{3,2,1,0:T(8,128)} %reshape.338) | data formatting | bytes 2097152 | tf_op jit(solution)/shard_map/reshape | solution.py:35
  1167.0 14.2 %copy.218 = f32[32,16,32,16]{3,1,2,0:T(8,128)} copy(f32[32,16,32,16]{3,2,1,0:T(8,128)} %reshape.339) | data formatting | bytes 2097152 | tf_op jit(solution)/shard_map/reshape | solution.py:35
  (244 shorter events, 247.6 us)
Async XLA Ops:
  7.2 166.4 %all-reduce.22.cloned.1.call-start = ((), (), s32[]{:S(2)}) async-start(), calls=%async_computation | async-start | bytes 8388608 | tf_op jit(solution)/shard_map/psum | solution.py:81
  9.7 2.7 copy-start.22
  28.2 737.5 %all-reduce.24.cloned.1.call-start = ((), (), s32[]{:S(2)}) async-start(), calls=%async_computation.1 | async-start | bytes 2097152 | tf_op jit(solution)/shard_map/psum | solution.py:91
  28.2 527.1 %copy-start.4 = (s32[128]{0:T(128)}, s32[128]{0:T(128)S(1)}, u32[]{:S(2)}) copy-start(s32[128]{0:T(128)S(1)} %or_bitcast_fusion.6) | copy-start | bytes 1540
  28.3 551.8 %copy-start.6 = (s32[64]{0:T(128)}, s32[64]{0:T(128)S(1)}, u32[]{:S(2)}) copy-start(s32[64]{0:T(128)S(1)} %or_bitcast_fusion.5) | copy-start | bytes 772
  28.3 573.7 %copy-start.15 = (s32[32]{0:T(128)}, s32[32]{0:T(128)S(1)}, u32[]{:S(2)}) copy-start(s32[32]{0:T(128)S(1)} %or_bitcast_fusion.4) | copy-start | bytes 388
  28.3 583.9 %copy-start.17 = (s32[16]{0:T(128)}, s32[16]{0:T(128)S(1)}, u32[]{:S(2)}) copy-start(s32[16]{0:T(128)S(1)} %or_bitcast_fusion.3) | copy-start | bytes 196
  28.3 590.8 %copy-start.20 = (s32[8]{0:T(128)}, s32[8]{0:T(128)S(1)}, u32[]{:S(2)}) copy-start(s32[8]{0:T(128)S(1)} %or_bitcast_fusion.2) | copy-start | bytes 100
  28.4 595.0 %copy-start.23 = (s32[4]{0:T(128)}, s32[4]{0:T(128)S(1)}, u32[]{:S(2)}) copy-start(s32[4]{0:T(128)S(1)} %or_bitcast_fusion.1) | copy-start | bytes 52
  28.4 485.6 %copy-start.2 = (s32[256,1]{0,1:T(1,128)}, s32[256,1]{0,1:T(1,128)S(1)}, u32[]{:S(2)}) copy-start(s32[256,1]{0,1:T(1,128)S(1)} %shift-left_or_fusion.1) | copy-start | bytes 3076
  28.4 244.4 %copy-start = (s32[512,1]{0,1:T(1,128)}, s32[512,1]{0,1:T(1,128)S(1)}, u32[]{:S(2)}) copy-start(s32[512,1]{0,1:T(1,128)S(1)} %shift-left_or_fusion) | copy-start | bytes 6148
  184.7 1.0 copy-start.10
  632.0 1.3 copy-start.25
  765.7 1.8 copy-start.8
  767.7 84.6 %copy-start.1 = (s32[512,1]{0,1:T(1,128)S(1)}, s32[512,1]{0,1:T(1,128)}, u32[]{:S(2)}) copy-start(s32[512,1]{0,1:T(1,128)} %copy-done) | copy-start | bytes 6148
  986.3 107.3 %copy-start.3 = (s32[256,1]{0,1:T(1,128)S(1)}, s32[256,1]{0,1:T(1,128)}, u32[]{:S(2)}) copy-start(s32[256,1]{0,1:T(1,128)} %copy-done.2) | copy-start | bytes 3076
  1096.9 37.8 %copy-start.5 = (s32[128]{0:T(128)S(1)}, s32[128]{0:T(128)}, u32[]{:S(2)}) copy-start(s32[128]{0:T(128)} %copy-done.4) | copy-start | bytes 1540
  1138.9 20.3 %copy-start.7 = (s32[64]{0:T(128)S(1)}, s32[64]{0:T(128)}, u32[]{:S(2)}) copy-start(s32[64]{0:T(128)} %copy-done.6) | copy-start | bytes 772
  1167.0 14.2 %copy-start.16 = (s32[32]{0:T(128)S(1)}, s32[32]{0:T(128)}, u32[]{:S(2)}) copy-start(s32[32]{0:T(128)} %copy-done.15) | copy-start | bytes 388
  1186.0 5.4 copy-start.18
  1191.5 7.0 copy-start.21
  1198.5 6.7 copy-start.24
  1205.1 5.3 copy-start.9
  1210.6 1.7 copy-start.19
  (4 other events, 3.1 us)
Sparse Core Ops, SparseCore 0:
  28.3 145.2 all-reduce.21
  635.7 129.9 all-reduce.23
where the time goes:
time: 1230 us
  local copies, waits for them, and re-layouts  708 us (58%)
  waiting for transfers between devices  274 us (22%)
  other arithmetic  175 us (14%)
  matrix products  49 us (4%)
  between operations  21 us (2%)
    reshape x32, local copies, waits for them, and re-layouts, lower_inverse(): tiles = lower.reshape(count, 2 * width, count, 2 * width)  635 us
    another operation x29, other arithmetic, upper_factor(): return jnp.linalg.cholesky(matrix).T  158 us
    psum x1, waiting for transfers between devices, on_device(): sketch = lax.psum(partial_sketch, ('had', 'blk'))  145 us
    psum x1, waiting for transfers between devices, on_device(): summed = lax.psum(partial_gram, ('had', 'blk'))  129 us
    gather x16, local copies, waits for them, and re-layouts, lower_inverse(): diag_tiles = jnp.moveaxis(jnp.diagonal(tiles, axis1=0, axis2=2), -1, 0)  40.2 us
  transfers between devices with their start and end apart: 2, of which 2 were waited for; matrix products, arithmetic and copies ran while one was open for 0% of the time, Pallas kernels for 0%

commit v1 on v0

v1 whole, which is shorter than its diff:
```python
import math

import jax
import jax.numpy as jnp
from jax import lax
from jax.experimental import pallas as pl
from jax.experimental.pallas import tpu as pltpu
from jax.sharding import PartitionSpec as P

LH = 32
TILE = 128
STEP = 8
HIGHEST = lax.Precision.HIGHEST


def bit_parity(value):
    counted = jnp.zeros_like(value)
    for shift_count in range(16):
        counted = counted + jnp.bitwise_and(jnp.right_shift(value, shift_count), 1)
    return counted % 2


def factor_tile(tile_ref):
    sub = lax.broadcasted_iota(jnp.int32, (STEP, TILE), 0)
    for start in range(0, TILE, STEP):
        left = tile_ref[start:start + STEP, 0:TILE]
        right = tile_ref[start:start + STEP, TILE:2 * TILE]
        spread = [
            jnp.broadcast_to(left[:, start + j:start + j + 1], (STEP, TILE)) for j in range(STEP)
        ]
        entry = {}
        for j in range(STEP):
            for i in range(j, STEP):
                entry[i, j] = jnp.broadcast_to(spread[j][i:i + 1, :], (STEP, TILE))
        for j in range(STEP):
            pivot = entry[j, j]
            scale = lax.rsqrt(pivot)
            scale = scale * (1.5 - 0.5 * pivot * scale * scale)
            below = {}
            column = jnp.zeros((STEP, TILE), jnp.float32)
            for i in range(j + 1, STEP):
                below[i] = entry[i, j] * scale
                column = jnp.where(sub == i, below[i], column)
            for m in range(j + 1, STEP):
                for i in range(m, STEP):
                    entry[i, m] = entry[i, m] - below[i] * below[m]
            row_left = jnp.broadcast_to(left[j:j + 1, :], (STEP, TILE)) * scale
            row_right = jnp.broadcast_to(right[j:j + 1, :], (STEP, TILE)) * scale
            left = jnp.where(sub == j, row_left, left - column * row_left)
            right = jnp.where(sub == j, row_right, right - column * row_right)
        tile_ref[start:start + STEP, 0:TILE] = left
        tile_ref[start:start + STEP, TILE:2 * TILE] = right
        if start + STEP < TILE:
            both = jnp.concatenate([left, right], axis=1)
            change = lax.dot_general(
                left, both, (((0,), (0,)), ((), ())), precision=HIGHEST,
                preferred_element_type=jnp.float32,
            )
            tile_ref[start + STEP:, :] = tile_ref[start + STEP:, :] - change[start + STEP:, :]


def factor_kernel(scale, matrix_ref, factor_ref, inverse_ref, work, tile):
    order = matrix_ref.shape[0]
    work[:, 0:order] = matrix_ref[...] * scale
    first = lax.broadcasted_iota(jnp.int32, (order, order), 0)
    second = lax.broadcasted_iota(jnp.int32, (order, order), 1)
    work[:, order:] = jnp.where(first == second, 1.0, 0.0)
    tile_first = lax.broadcasted_iota(jnp.int32, (TILE, TILE), 0)
    tile_second = lax.broadcasted_iota(jnp.int32, (TILE, TILE), 1)

    def step(which, carry):
        base = pl.multiple_of(which * TILE, TILE)
        rows = pl.ds(base, TILE)
        tile[:, 0:TILE] = work[rows, rows]
        tile[:, TILE:] = jnp.where(tile_first == tile_second, 1.0, 0.0)
        factor_tile(tile)
        solved = jnp.dot(
            tile[:, TILE:], work[rows, :], precision=HIGHEST, preferred_element_type=jnp.float32
        )
        work[rows, :] = solved
        for other in range(1, order // TILE):
            @pl.when(other > which)
            def _():
                part = slice(other * TILE, (other + 1) * TILE)
                work[part, :] = work[part, :] - lax.dot_general(
                    work[rows, part], work[rows, :], (((0,), (0,)), ((), ())),
                    precision=HIGHEST, preferred_element_type=jnp.float32,
                )
        return carry

    lax.fori_loop(0, order // TILE, step, 0)
    factor_ref[...] = jnp.where(first <= second, work[:, 0:order], 0.0)
    inverse_ref[...] = work[:, order:].astype(jnp.bfloat16)


def factor_and_inverse(matrix, scale, interpret=False):
    order = matrix.shape[0]

    def body(*refs):
        factor_kernel(scale, *refs)

    return pl.pallas_call(
        body,
        out_shape=(
            jax.ShapeDtypeStruct((order, order), jnp.float32),
            jax.ShapeDtypeStruct((order, order), jnp.bfloat16),
        ),
        in_specs=[pl.BlockSpec(memory_space=pltpu.VMEM)],
        out_specs=(pl.BlockSpec(memory_space=pltpu.VMEM),) * 2,
        scratch_shapes=[
            pltpu.VMEM((order, 2 * order), jnp.float32),
            pltpu.VMEM((TILE, 2 * TILE), jnp.float32),
        ],
        interpret=interpret,
    )(matrix)


def sample_kernel(panel_ref, flips_ref, group_ref, index_ref, weight_ref, out_ref, signed, picks):
    rows = panel_ref.shape[0]
    count = group_ref.shape[0]

    @pl.when(pl.program_id(0) == 0)
    def _():
        signed[...] = panel_ref[...] * flips_ref[...].astype(jnp.bfloat16)

    lane = lax.broadcasted_iota(jnp.int32, (count, TILE), 1)
    common = jnp.bitwise_and(jnp.broadcast_to(index_ref[...], (count, TILE)), lane)
    common = jnp.bitwise_xor(common, jnp.right_shift(common, 4))
    common = jnp.bitwise_xor(common, jnp.right_shift(common, 2))
    common = jnp.bitwise_xor(common, jnp.right_shift(common, 1))
    sign = (1 - 2 * jnp.bitwise_and(common, 1)).astype(jnp.float32)
    away = jnp.broadcast_to(group_ref[...], (count, TILE)) - jnp.right_shift(lane, 5)
    per_tile = TILE // LH
    for tile in range(rows // TILE):
        picks[:, tile * TILE:(tile + 1) * TILE] = jnp.where(
            away == tile * per_tile, sign, 0.0
        ).astype(jnp.bfloat16)
    out_ref[...] = weight_ref[...] * jnp.dot(
        picks[...], signed[...], preferred_element_type=jnp.float32
    )


def sample(panel, flips, groups, indices, weights, interpret=False):
    rows, columns = panel.shape
    total = groups.shape[0]
    count = 256
    narrow = pl.BlockSpec((count, 1), lambda i: (i, 0))
    return pl.pallas_call(
        sample_kernel,
        grid=(total // count,),
        out_shape=jax.ShapeDtypeStruct((total, columns), jnp.float32),
        in_specs=[
            pl.BlockSpec((rows, columns), lambda i: (0, 0)),
            pl.BlockSpec((rows, 1), lambda i: (0, 0)),
            narrow, narrow, narrow,
        ],
        out_specs=pl.BlockSpec((count, columns), lambda i: (i, 0)),
        scratch_shapes=[
            pltpu.VMEM((rows, columns), jnp.bfloat16),
            pltpu.VMEM((count, rows), jnp.bfloat16),
        ],
        interpret=interpret,
    )(panel, flips, groups, indices, weights)


def local_sketch(panel, signs, picks, my_group, factor, interpret=False):
    rows_dev = panel.shape[0]
    owners = picks // rows_dev
    offsets = picks % rows_dev
    parity = bit_parity(jnp.bitwise_and(owners, my_group))
    weights = (1 - 2 * parity).astype(jnp.float32) * factor
    flips = (1 - 2 * signs).astype(jnp.float32)
    return sample(
        panel, flips[:, None], (offsets // LH)[:, None], (offsets % LH)[:, None],
        weights[:, None], interpret,
    )


def on_device(panel, signs, sample_rows):
    n_had = lax.axis_size("had")
    n_blk = lax.axis_size("blk")
    my_group = lax.axis_index("had")
    rows_dev, columns = panel.shape
    sketch_count = sample_rows.shape[1]
    factor = 1.0 / math.sqrt(n_had * LH * sketch_count * n_blk)
    partial_sketch = local_sketch(panel, signs, sample_rows[0], my_group, factor)
    sketch = lax.psum(partial_sketch, ("had", "blk"))
    sketch_gram = jnp.dot(
        sketch.T, sketch, precision=HIGHEST, preferred_element_type=jnp.float32
    )
    r_sketch, sketch_inverse = factor_and_inverse(sketch_gram, 1.0)
    across = (((1,), (1,)), ((), ()))
    whitened = lax.dot_general(
        panel, sketch_inverse, across, preferred_element_type=jnp.float32
    ).astype(jnp.bfloat16)
    partial_gram = jnp.einsum("rk,rj->kj", whitened, whitened, preferred_element_type=jnp.float32)
    summed = lax.psum(partial_gram, ("had", "blk"))
    r_gram, gram_inverse = factor_and_inverse(summed, 1.0 / (rows_dev * n_had * n_blk))
    q_panel = lax.dot_general(
        whitened, gram_inverse, across, preferred_element_type=jnp.float32
    ).astype(jnp.bfloat16)
    return (q_panel, r_sketch, r_gram)


def solution(mesh):
    placed = (P(("had", "blk"), None), P(("had", "blk")), P("blk", None))
    return jax.shard_map(
        on_device,
        mesh=mesh,
        in_specs=placed,
        out_specs=(P(("had", "blk"), None), P(), P()),
        check_vma=False,
    )
```

time: 1230 us -> 421 us (0.34)
  local copies, waits for them, and re-layouts: 708 us -> 3.73 us
  other arithmetic: 175 us -> 6.78 us
  Pallas kernels: 0 us -> 101 us
  matrix products: 49 us -> 19.5 us
    reshape x32 -> x0, local copies, waits for them, and re-layouts: 635 us -> none  [lower_inverse(): tiles = lower.reshape(count, 2 * width, count, 2 * width)]
    another operation x29 -> x0, other arithmetic: 158 us -> none  [upper_factor(): return jnp.linalg.cholesky(matrix).T]
    pallas_call x0 -> x3, Pallas kernels: none -> 101 us  [the longest x2 90.2 us: factor_and_inverse(): pl.pallas_call(body, out_shape=(jax.ShapeDtypeStruct((order, order), jnp....]
    gather x19 -> x0, local copies, waits for them, and re-layouts: 61.2 us -> none  [the longest x16 40.2 us: lower_inverse(): diag_tiles = jnp.moveaxis(jnp.diagonal(tiles, axis1=0, axis2=2), -1, 0)]
    dot_general x36 -> x3, matrix products: 39.5 us -> 17.3 us  [the longest x1 11.3 us: on_device(): jnp.dot(sketch.T, sketch, precision=HIGHEST, preferred_element_type=jnp.f...]
where the time goes in v1:
time: 421 us
  waiting for transfers between devices  275 us (65%)
  Pallas kernels  101 us (24%)
  matrix products  19.5 us (5%)
  between operations  14.1 us (3%)
  other arithmetic  6.78 us (2%)
    psum x1, waiting for transfers between devices, on_device(): sketch = lax.psum(partial_sketch, ('had', 'blk'))  145 us
    psum x1, waiting for transfers between devices, on_device(): summed = lax.psum(partial_gram, ('had', 'blk'))  130 us
    pallas_call x2, Pallas kernels, factor_and_inverse(): pl.pallas_call(body, out_shape=(jax.ShapeDtypeStruct((order, order), jnp....  90.2 us
    dot_general x1, matrix products, on_device(): jnp.dot(sketch.T, sketch, precision=HIGHEST, preferred_element_type=jnp.f...  11.3 us
    pallas_call x1, Pallas kernels, sample(): pl.pallas_call(sample_kernel, grid=(total // count,), out_shape=jax.Shape...  10.9 us
  transfers between devices with their start and end apart: 2, of which 2 were waited for; matrix products, arithmetic and copies ran while one was open for 0% of the time, Pallas kernels for 0%

profile of v1, /device:TPU:0, one launch (start us, length us, event | category | flops | bytes accessed | tf_op | source)
XLA Modules:
  0.0 420.9 jit_solution(15331636978177630264)
XLA Ops:
  7.2 0.0 all-reduce.3.cloned.1.call-start
  7.2 0.7 subtract_convert_fusion
  7.9 1.3 copy.15.flips_ref
  9.3 1.1 copy.11
  10.3 2.6 add_select_fusion.2
  12.9 3.5 fusion.5.weight_ref
  16.4 10.9 %shard_map.58 = f32[2048,512]{1,0:T(8,128)} custom-call(bf16[2048,512]{1,0:T(8,128)(2,1)} %panel_ref.1, f32[2048,1]{1,0:T(8,128)} %copy.15.flips_ref, s32[2048,1]{1,0:T(8,128)} %get-tuple-element.12.group_ref, s32[2048,1]{1,0:T(8,128)} %get-tuple-element.11.index_ref, f32[2048,1]{1,0:T(8,128)} %fusion.5.weight_ref), custom_call_target="tpu_custom_call" | custom-call | tf_op jit(solution)/shard_map/pallas_call | solution.py:148
  27.3 0.0 all-reduce.3.cloned.1.call-update
  27.4 0.0 copy-start
  27.4 0.2 all-reduce.5.cloned.1.call-start
  27.6 145.2 %all-reduce.3.cloned.1.call-done = f32[2048,512]{1,0:T(8,128)} async-done(((f32[2048,512]{1,0:T(8,128)}), f32[2048,512]{1,0:T(8,128)}) %all-reduce.3.cloned.1.call-update) | async-done | bytes 4194320 | tf_op jit(solution)/shard_map/psum | solution.py:187
  172.8 11.3 %fusion.10.refs_0_ = f32[512,512]{1,0:T(8,128)} fusion(f32[2048,512]{1,0:T(8,128)} %all-reduce.3.cloned.1.call-done), kind=kOutput, calls=%fused_computation.28 | convolution fusion | flops 6442450944 | bytes 5242880 | tf_op jit(solution)/shard_map/dot_general | solution.py:188
  184.1 45.2 %shard_map.59 = (f32[512,512]{1,0:T(8,128)}, bf16[512,512]{1,0:T(8,128)(2,1)}) custom-call(f32[512,512]{1,0:T(8,128)} %fusion.10.refs_0_), custom_call_target="tpu_custom_call" | custom-call | tf_op jit(solution)/shard_map/pallas_call | solution.py:102
  229.3 0.0 copy-done
  229.3 2.3 convolution_convert_fusion.1
  231.7 0.0 copy-start.1
  231.7 1.3 copy-done.1
  233.0 2.3 fusion.11
  235.2 0.0 copy-start.2
  235.2 0.0 all-reduce.5.cloned.1.call-update
  235.3 130.1 %all-reduce.5.cloned.1.call-done.refs_0_ = f32[512,512]{1,0:T(8,128)} async-done(((f32[512,512]{1,0:T(8,128)}), f32[512,512]{1,0:T(8,128)}) %all-reduce.5.cloned.1.call-update) | async-done | bytes 1048592 | tf_op jit(solution)/shard_map/psum | solution.py:197
  365.4 45.0 %shard_map.60 = (f32[512,512]{1,0:T(8,128)}, bf16[512,512]{1,0:T(8,128)(2,1)}) custom-call(f32[512,512]{1,0:T(8,128)} %all-reduce.5.cloned.1.call-done.refs_0_), custom_call_target="tpu_custom_call" | custom-call | tf_op jit(solution)/shard_map/pallas_call | solution.py:102
  410.4 0.0 copy-done.2
  410.4 3.7 convolution_convert_fusion
Async XLA Ops:
  7.2 165.7 %all-reduce.3.cloned.1.call-start = ((), (), s32[]{:S(2)}) async-start(), calls=%async_computation | async-start | bytes 8388608 | tf_op jit(solution)/shard_map/psum | solution.py:187
  27.4 202.0 %copy-start = (bf16[2048,512]{1,0:T(8,128)(2,1)S(1)}, bf16[2048,512]{1,0:T(8,128)(2,1)}, u32[]{:S(2)}) copy-start(bf16[2048,512]{1,0:T(8,128)(2,1)} %panel_ref.1) | copy-start | bytes 6291460
  27.4 338.0 %all-reduce.5.cloned.1.call-start = ((), (), s32[]{:S(2)}) async-start(), calls=%async_computation.1 | async-start | bytes 2097152 | tf_op jit(solution)/shard_map/psum | solution.py:197
  231.7 1.3 copy-start.1
  235.2 175.2 %copy-start.2 = (bf16[512,2048]{1,0:T(8,128)(2,1)S(1)}, bf16[512,2048]{1,0:T(8,128)(2,1)}, u32[]{:S(2)}) copy-start(bf16[512,2048]{1,0:T(8,128)(2,1)} %copy-done.1) | copy-start | bytes 6291460
Sparse Core Ops, SparseCore 0:
  27.5 145.2 all-reduce.2
  235.4 129.9 all-reduce.4

commit v2 on v1

--- a/solution.py
+++ b/solution.py
@@ -176,6 +176,237 @@
     )
 
 
+def mesh_bits(n_had, n_blk):
+    bits = []
+    for axis, size in (("blk", n_blk), ("had", n_had)):
+        mask = 1
+        while mask < size:
+            bits.append((axis, mask))
+            mask *= 2
+    return bits
+
+
+def stream_orders(count):
+    plain = list(range(count))
+    swapped = list(plain)
+    if count > 2:
+        swapped[1], swapped[2] = swapped[2], swapped[1]
+    return plain, swapped
+
+
+def halving_count(rows, count):
+    halvings = 0
+    while halvings < count and (rows >> (halvings + 1)) >= STEP:
+        halvings += 1
+    return halvings
+
+
+def recv_bases(rows, count):
+    halvings = halving_count(rows, count)
+    bases, base = [], 0
+    for stage in range(count):
+        bases.append(base)
+        base += rows >> min(stage + 1, halvings)
+    return bases, base
+
+
+class Exchange:
+    def __init__(self, bits, send_sem, recv_sem):
+        self.bits = bits
+        self.send_sem, self.recv_sem = send_sem, recv_sem
+        self.used = 0
+        self.mine, self.partner = [], []
+        place = {"had": lax.axis_index("had"), "blk": lax.axis_index("blk")}
+        for axis, mask in bits:
+            bit = (place[axis] // mask) % 2
+            other = dict(place)
+            other[axis] = place[axis] + mask * (1 - 2 * bit)
+            self.mine.append(bit)
+            self.partner.append((other["had"], other["blk"]))
+
+    def barrier(self):
+        barrier = pltpu.get_barrier_semaphore()
+        for partner in self.partner:
+            pl.semaphore_signal(
+                barrier, inc=1, device_id=partner, device_id_type=pl.DeviceIdType.MESH
+            )
+        pl.semaphore_wait(barrier, len(self.bits))
+
+    def start(self, which, source, target):
+        copy = pltpu.make_async_remote_copy(
+            src_ref=source, dst_ref=target,
+            send_sem=self.send_sem.at[self.used], recv_sem=self.recv_sem.at[self.used],
+            device_id=self.partner[which], device_id_type=pl.DeviceIdType.MESH,
+        )
+        self.used += 1
+        copy.start()
+        return copy
+
+    def scatter(self, source, acc, recv, orders, same_rows):
+        rows, columns = source.shape
+        width = columns // len(orders)
+        count = len(self.bits)
+        halvings = halving_count(rows, count)
+        bases, _ = recv_bases(rows, count)
+
+        def weight(place):
+            return rows >> (place + 1)
+
+        def plan(stream, stage):
+            order = orders[stream]
+            where = (lambda s: order[s]) if same_rows else (lambda s: s)
+            fixed = 0
+            for s in range(min(stage, halvings)):
+                fixed = fixed + self.mine[order[s]] * weight(where(s))
+            which = order[stage]
+            if stage >= halvings:
+                return which, [(fixed, fixed, 0, rows >> halvings)]
+            taken = [where(s) for s in range(stage + 1)]
+            deepest = max(taken)
+            offsets = [0]
+            for place in range(deepest):
+                if place not in taken:
+                    offsets = offsets + [o + weight(place) for o in offsets]
+            length = weight(deepest)
+            step = weight(where(stage))
+            bit = self.mine[which]
+            return which, [
+                (fixed + o + (1 - bit) * step, fixed + o + bit * step, n * length, length)
+                for n, o in enumerate(offsets)
+            ]
+
+        def begin(stream, stage):
+            which, pieces = plan(stream, stage)
+            held = source if stage == 0 else acc
+            lanes = slice(stream * width, (stream + 1) * width)
+            copies = []
+            for send, _, inside, length in pieces:
+                copies.append(self.start(
+                    which,
+                    held.at[pl.ds(pl.multiple_of(send, STEP), length), lanes],
+                    recv.at[pl.ds(bases[stage] + inside, length), lanes],
+                ))
+            return copies
+
+        def finish(stream, stage, copies):
+            _, pieces = plan(stream, stage)
+            held = source if stage == 0 else acc
+            lanes = slice(stream * width, (stream + 1) * width)
+            for copy, (_, keep, inside, length) in zip(copies, pieces):
+                copy.wait()
+                here = pl.ds(pl.multiple_of(keep, STEP), length)
+                there = pl.ds(bases[stage] + inside, length)
+                acc[here, lanes] = held[here, lanes] + recv[there, lanes]
+
+        streams = range(len(orders))
+        flying = [begin(stream, 0) for stream in streams]
+        for stage in range(count):
+            for stream in streams:
+                finish(stream, stage, flying[stream])
+                if stage + 1 < count:
+                    flying[stream] = begin(stream, stage + 1)
+        kept = []
+        for order in orders:
+            offset = 0
+            for s in range(halvings):
+                offset = offset + self.mine[order[s]] * weight(order[s] if same_rows else s)
+            kept.append(offset)
+        return kept
+
+    def gather(self, acc, out, orders, kept):
+        rows, columns = out.shape
+        width = columns // len(orders)
+        halvings = halving_count(rows, len(self.bits))
+        kept = list(kept)
+        flying = [None] * len(orders)
+        streams = range(len(orders))
+
+        def begin(stream, stage):
+            lanes = slice(stream * width, (stream + 1) * width)
+            region = pl.ds(pl.multiple_of(kept[stream], STEP), rows >> (stage + 1))
+            flying[stream] = self.start(
+                orders[stream][stage], out.at[region, lanes], out.at[region, lanes]
+            )
+
+        for stream in streams:
+            lanes = slice(stream * width, (stream + 1) * width)
+            region = pl.ds(pl.multiple_of(kept[stream], STEP), rows >> halvings)
+            out[region, lanes] = acc[region, lanes]
+            begin(stream, halvings - 1)
+        for stage in reversed(range(halvings)):
+            for stream in streams:
+                flying[stream].wait()
+                kept[stream] = kept[stream] - self.mine[orders[stream][stage]] * (rows >> (stage + 1))
+                if stage:
+                    begin(stream, stage - 1)
+
+
+def sketch_gram_sum(partial, n_had, n_blk):
+    rows, columns = partial.shape
+    bits = mesh_bits(n_had, n_blk)
+    count = len(bits)
+    orders = stream_orders(count)
+    own = rows >> count
+    copies = 8 * count + 8
+
+    def body(in_ref, out_ref, acc, recv, part, total, landed, send_sem, recv_sem):
+        exchange = Exchange(bits, send_sem, recv_sem)
+        exchange.barrier()
+        kept = exchange.scatter(in_ref, acc, recv, orders, True)
+        mine = acc[pl.ds(pl.multiple_of(kept[0], STEP), own), :]
+        part[...] = lax.dot_general(
+            mine, mine, (((0,), (0,)), ((), ())), precision=HIGHEST,
+            preferred_element_type=jnp.float32,
+        )
+        kept = exchange.scatter(part, total, landed, orders, False)
+        exchange.gather(total, out_ref, orders, kept)
+
+    return pl.pallas_call(
+        body,
+        out_shape=jax.ShapeDtypeStruct((columns, columns), jnp.float32),
+        in_specs=[pl.BlockSpec(memory_space=pltpu.VMEM)],
+        out_specs=pl.BlockSpec(memory_space=pltpu.VMEM),
+        scratch_shapes=[
+            pltpu.VMEM((rows, columns), jnp.float32),
+            pltpu.VMEM((recv_bases(rows, count)[1], columns), jnp.float32),
+            pltpu.VMEM((columns, columns), jnp.float32),
+            pltpu.VMEM((columns, columns), jnp.float32),
+            pltpu.VMEM((recv_bases(columns, count)[1], columns), jnp.float32),
+            pltpu.SemaphoreType.DMA((copies,)),
+            pltpu.SemaphoreType.DMA((copies,)),
+        ],
+        compiler_params=pltpu.CompilerParams(collective_id=0, has_side_effects=True),
+    )(partial)
+
+
+def matrix_sum(partial, n_had, n_blk):
+    rows, columns = partial.shape
+    bits = mesh_bits(n_had, n_blk)
+    count = len(bits)
+    orders = stream_orders(count)
+    copies = 4 * count + 4
+
+    def body(in_ref, out_ref, total, landed, send_sem, recv_sem):
+        exchange = Exchange(bits, send_sem, recv_sem)
+        exchange.barrier()
+        kept = exchange.scatter(in_ref, total, landed, orders, False)
+        exchange.gather(total, out_ref, orders, kept)
+
+    return pl.pallas_call(
+        body,
+        out_shape=jax.ShapeDtypeStruct((rows, columns), jnp.float32),
+        in_specs=[pl.BlockSpec(memory_space=pltpu.VMEM)],
+        out_specs=pl.BlockSpec(memory_space=pltpu.VMEM),
+        scratch_shapes=[
+            pltpu.VMEM((rows, columns), jnp.float32),
+            pltpu.VMEM((recv_bases(rows, count)[1], columns), jnp.float32),
+            pltpu.SemaphoreType.DMA((copies,)),
+            pltpu.SemaphoreType.DMA((copies,)),
+        ],
+        compiler_params=pltpu.CompilerParams(collective_id=1, has_side_effects=True),
+    )(partial)
+
+
 def on_device(panel, signs, sample_rows):
     n_had = lax.axis_size("had")
     n_blk = lax.axis_size("blk")
@@ -184,17 +415,14 @@
     sketch_count = sample_rows.shape[1]
     factor = 1.0 / math.sqrt(n_had * LH * sketch_count * n_blk)
     partial_sketch = local_sketch(panel, signs, sample_rows[0], my_group, factor)
-    sketch = lax.psum(partial_sketch, ("had", "blk"))
-    sketch_gram = jnp.dot(
-        sketch.T, sketch, precision=HIGHEST, preferred_element_type=jnp.float32
-    )
+    sketch_gram = sketch_gram_sum(partial_sketch, n_had, n_blk)
     r_sketch, sketch_inverse = factor_and_inverse(sketch_gram, 1.0)
     across = (((1,), (1,)), ((), ()))
     whitened = lax.dot_general(
         panel, sketch_inverse, across, preferred_element_type=jnp.float32
     ).astype(jnp.bfloat16)
     partial_gram = jnp.einsum("rk,rj->kj", whitened, whitened, preferred_element_type=jnp.float32)
-    summed = lax.psum(partial_gram, ("had", "blk"))
+    summed = matrix_sum(partial_gram, n_had, n_blk)
     r_gram, gram_inverse = factor_and_inverse(summed, 1.0 / (rows_dev * n_had * n_blk))
     q_panel = lax.dot_general(
         whitened, gram_inverse, across, preferred_element_type=jnp.float32

time: 421 us -> 234 us (0.56)
  waiting for transfers between devices: 275 us -> 0 us
  Pallas kernels: 101 us -> 214 us
  between operations: 14.1 us -> 0.68 us
  matrix products: 19.5 us -> 8.25 us
    psum x2 -> x0, waiting for transfers between devices: 275 us -> none  [the longest x1 145 us: on_device(): sketch = lax.psum(partial_sketch, ('had', 'blk'))]
    pallas_call x0 -> x2, Pallas kernels: none -> 113 us  [the longest x1 77.1 us: sketch_gram_sum(): pl.pallas_call(body, out_shape=jax.ShapeDtypeStruct((columns, columns), j...]
    dot_general x1 -> x0, matrix products: 11.3 us -> none  [on_device(): jnp.dot(sketch.T, sketch, precision=HIGHEST, preferred_element_type=jnp.f...]
  transfers between devices with their start and end apart: 2 -> 0, of which waited for: 2 -> 0; matrix products, arithmetic and copies ran while one was open for 0% -> 0% of each run, Pallas kernels for 0% -> 0%
where the time goes in v2:
time: 234 us; the launch traced here: 233 us
  Pallas kernels  214 us (91%)
  matrix products  8.25 us (4%)
  other arithmetic  6.81 us (3%)
  local copies, waits for them, and re-layouts  3.72 us (2%)
    pallas_call x2, Pallas kernels, factor_and_inverse(): pl.pallas_call(body, out_shape=(jax.ShapeDtypeStruct((order, order), jnp....  90.2 us
    pallas_call x1, Pallas kernels, sketch_gram_sum(): pl.pallas_call(body, out_shape=jax.ShapeDtypeStruct((columns, columns), j...  77.1 us
    pallas_call x1, Pallas kernels, matrix_sum(): pl.pallas_call(body, out_shape=jax.ShapeDtypeStruct((rows, columns), jnp....  35.7 us
    pallas_call x1, Pallas kernels, sample(): pl.pallas_call(sample_kernel, grid=(total // count,), out_shape=jax.Shape...  10.9 us

profile of v2, /device:TPU:0, one launch (start us, length us, event | category | flops | bytes accessed | tf_op | source)
XLA Modules:
  0.0 233.4 jit_solution(14439830318922342760)
XLA Ops:
  0.6 0.7 subtract_convert_fusion
  1.3 1.3 copy.15.flips_ref
  2.7 1.1 copy.11
  3.7 3.5 %fusion.5.weight_ref = f32[2048,1]{1,0:T(8,128)} fusion(s32[2048,1]{1,0:T(8,128)S(1)} %copy.11, s32[]{:T(128)S(6)} %axis_index.15), kind=kLoop, calls=%fused_computation.20 | loop fusion | flops 159744 | bytes 16388 | tf_op jit(solution)/shard_map/mul | solution.py:171
  7.3 2.6 %add_select_fusion.2 = (s32[2048,1]{1,0:T(8,128)}, s32[2048,1]{1,0:T(8,128)}) fusion(s32[2048,1]{1,0:T(8,128)S(1)} %copy.11), kind=kLoop, calls=%fused_computation.7 | loop fusion | flops 61440 | bytes 24576 | tf_op jit(solution)/shard_map/jit(remainder)/select_n | solution.py:174
  9.9 10.9 %shard_map.58.in_ref = f32[2048,512]{1,0:T(8,128)} custom-call(bf16[2048,512]{1,0:T(8,128)(2,1)} %panel_ref.1, f32[2048,1]{1,0:T(8,128)} %copy.15.flips_ref, s32[2048,1]{1,0:T(8,128)} %get-tuple-element.12.group_ref, s32[2048,1]{1,0:T(8,128)} %get-tuple-element.11.index_ref, f32[2048,1]{1,0:T(8,128)} %fusion.5.weight_ref), custom_call_target="tpu_custom_call" | custom-call | tf_op jit(solution)/shard_map/pallas_call | solution.py:148
  20.8 0.0 copy-start
  20.8 77.1 %shard_map.59.refs_0_ = f32[512,512]{1,0:T(8,128)} custom-call(f32[2048,512]{1,0:T(8,128)} %shard_map.58.in_ref), custom_call_target="tpu_custom_call" | custom-call | tf_op jit(solution)/shard_map/pallas_call | solution.py:364
  97.9 45.2 %shard_map.60 = (f32[512,512]{1,0:T(8,128)}, bf16[512,512]{1,0:T(8,128)(2,1)}) custom-call(f32[512,512]{1,0:T(8,128)} %shard_map.59.refs_0_), custom_call_target="tpu_custom_call" | custom-call | tf_op jit(solution)/shard_map/pallas_call | solution.py:102
  143.0 0.0 copy-done
  143.0 2.3 convolution_convert_fusion.1
  145.4 0.0 copy-start.1
  145.4 1.3 copy-done.1
  146.7 2.3 fusion.10.in_ref
  149.0 0.0 copy-start.2
  149.0 35.7 %shard_map.61.refs_0_ = f32[512,512]{1,0:T(8,128)} custom-call(f32[512,512]{1,0:T(8,128)} %fusion.10.in_ref), custom_call_target="tpu_custom_call" | custom-call | tf_op jit(solution)/shard_map/pallas_call | solution.py:395
  184.7 45.0 %shard_map.62 = (f32[512,512]{1,0:T(8,128)}, bf16[512,512]{1,0:T(8,128)(2,1)}) custom-call(f32[512,512]{1,0:T(8,128)} %shard_map.61.refs_0_), custom_call_target="tpu_custom_call" | custom-call | tf_op jit(solution)/shard_map/pallas_call | solution.py:102
  229.7 0.0 copy-done.2
  229.7 3.7 %convolution_convert_fusion = bf16[2048,512]{1,0:T(8,128)(2,1)} fusion(bf16[512,2048]{1,0:T(8,128)(2,1)S(1)} %copy-done.2, bf16[512,512]{1,0:T(8,128)(2,1)} %get-tuple-element.8), kind=kOutput, calls=%fused_computation | convolution fusion | flops 1074790400 | bytes 4718592 | tf_op jit(solution)/shard_map/dot_general | solution.py:427
Async XLA Ops:
  20.8 122.3 %copy-start = (bf16[2048,512]{1,0:T(8,128)(2,1)S(1)}, bf16[2048,512]{1,0:T(8,128)(2,1)}, u32[]{:S(2)}) copy-start(bf16[2048,512]{1,0:T(8,128)(2,1)} %panel_ref.1) | copy-start | bytes 6291460
  145.4 1.3 copy-start.1
  149.0 80.7 %copy-start.2 = (bf16[512,2048]{1,0:T(8,128)(2,1)S(1)}, bf16[512,2048]{1,0:T(8,128)(2,1)}, u32[]{:S(2)}) copy-start(bf16[512,2048]{1,0:T(8,128)(2,1)} %copy-done.1) | copy-start | bytes 6291460

commit v3 on v2

--- a/solution.py
+++ b/solution.py
@@ -10,53 +10,61 @@
 LH = 32
 TILE = 128
 STEP = 8
+SUPER = 32
 HIGHEST = lax.Precision.HIGHEST
-
-
-def bit_parity(value):
-    counted = jnp.zeros_like(value)
-    for shift_count in range(16):
-        counted = counted + jnp.bitwise_and(jnp.right_shift(value, shift_count), 1)
-    return counted % 2
 
 
 def factor_tile(tile_ref):
     sub = lax.broadcasted_iota(jnp.int32, (STEP, TILE), 0)
-    for start in range(0, TILE, STEP):
-        left = tile_ref[start:start + STEP, 0:TILE]
-        right = tile_ref[start:start + STEP, TILE:2 * TILE]
-        spread = [
-            jnp.broadcast_to(left[:, start + j:start + j + 1], (STEP, TILE)) for j in range(STEP)
-        ]
-        entry = {}
-        for j in range(STEP):
-            for i in range(j, STEP):
-                entry[i, j] = jnp.broadcast_to(spread[j][i:i + 1, :], (STEP, TILE))
-        for j in range(STEP):
-            pivot = entry[j, j]
-            scale = lax.rsqrt(pivot)
-            scale = scale * (1.5 - 0.5 * pivot * scale * scale)
-            below = {}
-            column = jnp.zeros((STEP, TILE), jnp.float32)
-            for i in range(j + 1, STEP):
-                below[i] = entry[i, j] * scale
-                column = jnp.where(sub == i, below[i], column)
-            for m in range(j + 1, STEP):
-                for i in range(m, STEP):
-                    entry[i, m] = entry[i, m] - below[i] * below[m]
-            row_left = jnp.broadcast_to(left[j:j + 1, :], (STEP, TILE)) * scale
-            row_right = jnp.broadcast_to(right[j:j + 1, :], (STEP, TILE)) * scale
-            left = jnp.where(sub == j, row_left, left - column * row_left)
-            right = jnp.where(sub == j, row_right, right - column * row_right)
-        tile_ref[start:start + STEP, 0:TILE] = left
-        tile_ref[start:start + STEP, TILE:2 * TILE] = right
-        if start + STEP < TILE:
-            both = jnp.concatenate([left, right], axis=1)
+    shape = (STEP, TILE)
+    for base in range(0, TILE, SUPER):
+        parts = SUPER // STEP
+        left = [tile_ref[base + p * STEP:base + (p + 1) * STEP, 0:TILE] for p in range(parts)]
+        right = [tile_ref[base + p * STEP:base + (p + 1) * STEP, TILE:] for p in range(parts)]
+        for now in range(parts):
+            start = base + now * STEP
+            rest = range(now + 1, parts)
+            spread = {
+                (p, j): jnp.broadcast_to(left[p][:, start + j:start + j + 1], shape)
+                for j in range(STEP) for p in range(now, parts)
+            }
+            entry = {
+                (i, j): jnp.broadcast_to(spread[now, j][i:i + 1, :], shape)
+                for j in range(STEP) for i in range(j, STEP)
+            }
+            for j in range(STEP):
+                pivot = entry[j, j]
+                scale = lax.rsqrt(pivot)
+                scale = scale * (1.5 - 0.5 * pivot * scale * scale)
+                below = {}
+                column = jnp.zeros(shape, jnp.float32)
+                for i in range(j + 1, STEP):
+                    below[i] = entry[i, j] * scale
+                    column = jnp.where(sub == i, below[i], column)
+                for m in range(j + 1, STEP):
+                    for i in range(m, STEP):
+                        entry[i, m] = entry[i, m] - below[i] * below[m]
+                row_left = jnp.broadcast_to(left[now][j:j + 1, :], shape) * scale
+                row_right = jnp.broadcast_to(right[now][j:j + 1, :], shape) * scale
+                left[now] = jnp.where(sub == j, row_left, left[now] - column * row_left)
+                right[now] = jnp.where(sub == j, row_right, right[now] - column * row_right)
+                for p in rest:
+                    outer = spread[p, j] * scale
+                    for m in range(j + 1, STEP):
+                        spread[p, m] = spread[p, m] - outer * below[m]
+                    left[p] = left[p] - outer * row_left
+                    right[p] = right[p] - outer * row_right
+        lefts = jnp.concatenate(left, axis=0)
+        rights = jnp.concatenate(right, axis=0)
+        tile_ref[base:base + SUPER, 0:TILE] = lefts
+        tile_ref[base:base + SUPER, TILE:] = rights
+        if base + SUPER < TILE:
+            both = jnp.concatenate([lefts, rights], axis=1)
             change = lax.dot_general(
-                left, both, (((0,), (0,)), ((), ())), precision=HIGHEST,
+                lefts, both, (((0,), (0,)), ((), ())), precision=HIGHEST,
                 preferred_element_type=jnp.float32,
             )
-            tile_ref[start + STEP:, :] = tile_ref[start + STEP:, :] - change[start + STEP:, :]
+            tile_ref[base + SUPER:, :] = tile_ref[base + SUPER:, :] - change[base + SUPER:, :]
 
 
 def factor_kernel(scale, matrix_ref, factor_ref, inverse_ref, work, tile):
@@ -115,65 +123,62 @@
     )(matrix)
 
 
-def sample_kernel(panel_ref, flips_ref, group_ref, index_ref, weight_ref, out_ref, signed, picks):
+def sample_kernel(factor, panel_ref, signs_ref, picks_ref, out_ref, signed, chosen):
     rows = panel_ref.shape[0]
-    count = group_ref.shape[0]
+    count = picks_ref.shape[0]
 
     @pl.when(pl.program_id(0) == 0)
     def _():
-        signed[...] = panel_ref[...] * flips_ref[...].astype(jnp.bfloat16)
-
+        flips = (1 - 2 * signs_ref[...]).astype(jnp.float32).astype(jnp.bfloat16)
+        signed[...] = panel_ref[...] * flips
+
+    def sign_of(value, shifts):
+        for shift in shifts:
+            value = jnp.bitwise_xor(value, jnp.right_shift(value, shift))
+        return (1 - 2 * jnp.bitwise_and(value, 1)).astype(jnp.float32)
+
+    picks = jnp.broadcast_to(picks_ref[...], (count, TILE))
     lane = lax.broadcasted_iota(jnp.int32, (count, TILE), 1)
-    common = jnp.bitwise_and(jnp.broadcast_to(index_ref[...], (count, TILE)), lane)
-    common = jnp.bitwise_xor(common, jnp.right_shift(common, 4))
-    common = jnp.bitwise_xor(common, jnp.right_shift(common, 2))
-    common = jnp.bitwise_xor(common, jnp.right_shift(common, 1))
-    sign = (1 - 2 * jnp.bitwise_and(common, 1)).astype(jnp.float32)
-    away = jnp.broadcast_to(group_ref[...], (count, TILE)) - jnp.right_shift(lane, 5)
-    per_tile = TILE // LH
+    owners = picks // rows
+    offsets = picks - owners * rows
+    groups = offsets // LH
+    indices = offsets - groups * LH
+    sign = sign_of(jnp.bitwise_and(indices, lane), (4, 2, 1))
+    outer = sign_of(jnp.bitwise_and(owners, lax.axis_index("had")), (8, 4, 2, 1))
+    weights = outer[:, 0:1] * factor
+    away = groups - lane // LH
     for tile in range(rows // TILE):
-        picks[:, tile * TILE:(tile + 1) * TILE] = jnp.where(
-            away == tile * per_tile, sign, 0.0
+        chosen[:, tile * TILE:(tile + 1) * TILE] = jnp.where(
+            away == tile * (TILE // LH), sign, 0.0
         ).astype(jnp.bfloat16)
-    out_ref[...] = weight_ref[...] * jnp.dot(
-        picks[...], signed[...], preferred_element_type=jnp.float32
+    out_ref[...] = weights * jnp.dot(
+        chosen[...], signed[...], preferred_element_type=jnp.float32
     )
 
 
-def sample(panel, flips, groups, indices, weights, interpret=False):
+def local_sketch(panel, signs, picks, factor):
     rows, columns = panel.shape
-    total = groups.shape[0]
+    total = picks.shape[0]
     count = 256
-    narrow = pl.BlockSpec((count, 1), lambda i: (i, 0))
+
+    def body(*refs):
+        sample_kernel(factor, *refs)
+
     return pl.pallas_call(
-        sample_kernel,
+        body,
         grid=(total // count,),
         out_shape=jax.ShapeDtypeStruct((total, columns), jnp.float32),
         in_specs=[
             pl.BlockSpec((rows, columns), lambda i: (0, 0)),
             pl.BlockSpec((rows, 1), lambda i: (0, 0)),
-            narrow, narrow, narrow,
+            pl.BlockSpec((count, 1), lambda i: (i, 0)),
         ],
         out_specs=pl.BlockSpec((count, columns), lambda i: (i, 0)),
         scratch_shapes=[
             pltpu.VMEM((rows, columns), jnp.bfloat16),
             pltpu.VMEM((count, rows), jnp.bfloat16),
         ],
-        interpret=interpret,
-    )(panel, flips, groups, indices, weights)
-
-
-def local_sketch(panel, signs, picks, my_group, factor, interpret=False):
-    rows_dev = panel.shape[0]
-    owners = picks // rows_dev
-    offsets = picks % rows_dev
-    parity = bit_parity(jnp.bitwise_and(owners, my_group))
-    weights = (1 - 2 * parity).astype(jnp.float32) * factor
-    flips = (1 - 2 * signs).astype(jnp.float32)
-    return sample(
-        panel, flips[:, None], (offsets // LH)[:, None], (offsets % LH)[:, None],
-        weights[:, None], interpret,
-    )
+    )(panel, signs[:, None], picks[:, None])
 
 
 def mesh_bits(n_had, n_blk):
@@ -410,11 +415,10 @@
 def on_device(panel, signs, sample_rows):
     n_had = lax.axis_size("had")
     n_blk = lax.axis_size("blk")
-    my_group = lax.axis_index("had")
     rows_dev, columns = panel.shape
     sketch_count = sample_rows.shape[1]
     factor = 1.0 / math.sqrt(n_had * LH * sketch_count * n_blk)
-    partial_sketch = local_sketch(panel, signs, sample_rows[0], my_group, factor)
+    partial_sketch = local_sketch(panel, signs, sample_rows[0], factor)
     sketch_gram = sketch_gram_sum(partial_sketch, n_had, n_blk)
     r_sketch, sketch_inverse = factor_and_inverse(sketch_gram, 1.0)
     across = (((1,), (1,)), ((), ()))

time: 234 us -> 194 us (0.83)
  Pallas kernels: 214 us -> 180 us
  other arithmetic: 6.81 us -> 0 us
    pallas_call x2, Pallas kernels: 90.2 us -> 55.6 us  [factor_and_inverse(): pl.pallas_call(body, out_shape=(jax.ShapeDtypeStruct((order, order), jnp....]
    mul x1 -> x0, other arithmetic: 3.54 us -> none  [local_sketch(): weights = (1 - 2 * parity).astype(jnp.float32) * factor]
    select_n x1 -> x0, other arithmetic: 2.57 us -> none  [local_sketch(): offsets % LH]
where the time goes in v3:
time: 194 us
  Pallas kernels  180 us (93%)
  matrix products  8.24 us (4%)
  local copies, waits for them, and re-layouts  5.39 us (3%)
    pallas_call x1, Pallas kernels, sketch_gram_sum(): pl.pallas_call(body, out_shape=jax.ShapeDtypeStruct((columns, columns), j...  77.1 us
    pallas_call x2, Pallas kernels, factor_and_inverse(): pl.pallas_call(body, out_shape=(jax.ShapeDtypeStruct((order, order), jnp....  55.6 us
    pallas_call x1, Pallas kernels, matrix_sum(): pl.pallas_call(body, out_shape=jax.ShapeDtypeStruct((rows, columns), jnp....  35.7 us
    pallas_call x1, Pallas kernels, local_sketch(): pl.pallas_call(body, grid=(total // count,), out_shape=jax.ShapeDtypeStru...  11.2 us

profile of v3, /device:TPU:0, one launch (start us, length us, event | category | flops | bytes accessed | tf_op | source)
XLA Modules:
  0.0 193.9 jit_solution(11908360781252208391)
XLA Ops:
  0.6 2.0 %copy.6.refs_1_ = s32[2048,1]{1,0:T(8,128)} copy(s32[2048,1]{0,1:T(1,128)} %bitcast.8) | data formatting | bytes 16384 | tf_op jit(solution)/shard_map/broadcast_in_dim | solution.py:181
  2.7 2.0 %copy.7.refs_2_ = s32[2048,1]{1,0:T(8,128)} copy(s32[2048,1]{0,1:T(1,128)} %bitcast.9) | data formatting | bytes 16384 | tf_op jit(solution)/shard_map/broadcast_in_dim;squeeze | solution.py:181
  4.7 11.2 %shard_map.58.in_ref = f32[2048,512]{1,0:T(8,128)} custom-call(bf16[2048,512]{1,0:T(8,128)(2,1)} %refs_0_.1, s32[2048,1]{1,0:T(8,128)} %copy.6.refs_1_, s32[2048,1]{1,0:T(8,128)} %copy.7.refs_2_), custom_call_target="tpu_custom_call" | custom-call | tf_op jit(solution)/shard_map/pallas_call | solution.py:167
  15.9 0.0 copy-start
  15.9 77.1 %shard_map.59.refs_0_ = f32[512,512]{1,0:T(8,128)} custom-call(f32[2048,512]{1,0:T(8,128)} %shard_map.58.in_ref), custom_call_target="tpu_custom_call" | custom-call | tf_op jit(solution)/shard_map/pallas_call | solution.py:369
  93.0 27.7 %shard_map.60 = (f32[512,512]{1,0:T(8,128)}, bf16[512,512]{1,0:T(8,128)(2,1)}) custom-call(f32[512,512]{1,0:T(8,128)} %shard_map.59.refs_0_), custom_call_target="tpu_custom_call" | custom-call | tf_op jit(solution)/shard_map/pallas_call | solution.py:110
  120.7 0.0 copy-done
  120.7 2.3 %convolution_convert_fusion.1 = bf16[512,2048]{1,0:T(8,128)(2,1)S(1)} fusion(bf16[512,512]{1,0:T(8,128)(2,1)} %get-tuple-element.7, bf16[2048,512]{1,0:T(8,128)(2,1)S(1)} %copy-done), kind=kOutput, calls=%fused_computation.1 | convolution fusion | flops 1074790400 | bytes 4718592 | tf_op jit(solution)/shard_map/dot_general | solution.py:425
  123.0 0.0 copy-start.1
  123.0 1.3 copy-done.1
  124.3 2.2 %fusion.in_ref = f32[512,512]{1,0:T(8,128)} fusion(bf16[512,2048]{1,0:T(8,128)(2,1)S(1)} %convolution_convert_fusion.1), kind=kOutput, calls=%fused_computation.2 | convolution fusion | flops 1073741824 | bytes 3145728 | tf_op jit(solution)/shard_map/rk,rj->kj/dot_general | solution.py:428
  126.6 0.0 copy-start.2
  126.6 35.7 %shard_map.61.refs_0_ = f32[512,512]{1,0:T(8,128)} custom-call(f32[512,512]{1,0:T(8,128)} %fusion.in_ref), custom_call_target="tpu_custom_call" | custom-call | tf_op jit(solution)/shard_map/pallas_call | solution.py:400
  162.3 27.9 %shard_map.62 = (f32[512,512]{1,0:T(8,128)}, bf16[512,512]{1,0:T(8,128)(2,1)}) custom-call(f32[512,512]{1,0:T(8,128)} %shard_map.61.refs_0_), custom_call_target="tpu_custom_call" | custom-call | tf_op jit(solution)/shard_map/pallas_call | solution.py:110
  190.2 0.0 copy-done.2
  190.2 3.7 %convolution_convert_fusion = bf16[2048,512]{1,0:T(8,128)(2,1)} fusion(bf16[512,2048]{1,0:T(8,128)(2,1)S(1)} %copy-done.2, bf16[512,512]{1,0:T(8,128)(2,1)} %get-tuple-element.8), kind=kOutput, calls=%fused_computation | convolution fusion | flops 1074790400 | bytes 4718592 | tf_op jit(solution)/shard_map/dot_general | solution.py:431
Async XLA Ops:
  15.9 104.8 %copy-start = (bf16[2048,512]{1,0:T(8,128)(2,1)S(1)}, bf16[2048,512]{1,0:T(8,128)(2,1)}, u32[]{:S(2)}) copy-start(bf16[2048,512]{1,0:T(8,128)(2,1)} %refs_0_.1) | copy-start | bytes 6291460
  123.0 1.3 copy-start.1
  126.6 63.7 %copy-start.2 = (bf16[512,2048]{1,0:T(8,128)(2,1)S(1)}, bf16[512,2048]{1,0:T(8,128)(2,1)}, u32[]{:S(2)}) copy-start(bf16[512,2048]{1,0:T(8,128)(2,1)} %copy-done.1) | copy-start | bytes 6291460
